TPU v7x, 32 devices: a whole 2x2x4 slice. The times are simulated.
32 devices in a mesh: groups: 2 (over y), mem: 4 (over x, core), heads: 4 (over z).
Axes of the slice: x: 2, y: 2, z: 4, core: 2. Of those that a mesh axis runs over, the one named last changes fastest.
Arguments:
- hidden: bfloat16 [32, 8192], P(('groups', 'heads')), parts along dimension 0, may hold values from -6 to 6
- norm_gain: bfloat16 [8192], P('mem'), may hold values from 0.5 to 1.5
- q_weight: bfloat16 [8192, 8192], P('mem', 'heads'), may hold values from -0.0625 to 0.0625
- k_weight: bfloat16 [8192, 1024], P('mem', 'heads'), may hold values from -1 to 1, as said below
- v_weight: bfloat16 [8192, 1024], P('mem', 'heads'), may hold values from -1 to 1, as said below
- o_weight: bfloat16 [8192, 8192], P('heads', 'mem'), may hold values from -0.0625 to 0.0625
- k_cache: bfloat16 [384, 8, 128, 128], P(('groups', 'mem'), 'heads'), parts along dimension 0, may hold values from -40 to 40, as said below
- v_cache: bfloat16 [384, 8, 128, 128], P(('groups', 'mem'), 'heads'), parts along dimension 0, may hold values from -6 to 6, as said below
- page_table: int32 [16, 24], P('groups'), parts along dimension 0, may hold values from 0 to 191, as said below
- attend_list: int32 [16, 8], P('groups'), parts along dimension 0, may hold values from 0 to 23, as said below
- lengths: int32 [16], P('groups'), parts along dimension 0, may hold values from 1409 to 3072, as said below
Outputs:
- layer_out: bfloat16 [32, 8192], P(('groups', 'heads'), 'mem'), parts along dimension 0
There are 2 independent parts, one for each index of `groups`. A program takes and returns all parts, laid end to end along the dimension named above; an argument that names none is the same for every part. Nothing has to cross between parts.
Inputs may be any that keep to these rules, and one draw needn't show every extreme that they name: `page_table`: A permutation of the pool slots 0 to 191 laid out as 8 rows of 24. The blocks named by attend_list lie at most 32 in any one range of slots m * 48 to (m + 1) * 48 - 1, and exactly 32 in some such range. `attend_list`: each row names 8 distinct blocks, all below ceil(lengths[r] / 128), among them its last block ceil(lengths[r] / 128) - 1. `lengths`: some row holds 3072 steps. `k_cache`: each key-value head is stored 1 times, the copies equal. `v_cache`: each key-value head is stored 1 times, the copies equal. `k_weight`: the 1 column blocks of each key-value head are equal. `v_weight`: the 1 column blocks of each key-value head are equal.
All inputs are finite; a program needn't handle non-finite values.
Results may differ from a plain program's by a relative error of at most 0.007.
The roundings to bfloat16 on the way count: a program that leaves them out, or rounds other values in their place, can miss the bound.
Values may be sent and summed in bfloat16 or wider, within the bound.
A program may use at most 64 MiB of HBM per device.

v0:
```python
import jax
import jax.numpy as jnp
from jax import lax
from jax.sharding import PartitionSpec as P

NEG_FILL = -1e30
EPSILON = 1e-05


def fold_owners(running, shard_piece):
    piece_peak, piece_total, piece_accum = shard_piece
    run_peak, run_total, run_accum = running
    joint_peak = jnp.maximum(run_peak, jnp.max(piece_peak, axis=0))
    piece_factor = jnp.exp(piece_peak - joint_peak[None])
    joint_total = jnp.sum(piece_total * piece_factor, axis=0)
    joint_accum = jnp.sum(piece_accum * piece_factor[..., None], axis=0)
    return (joint_peak, joint_total, joint_accum)


def shards(
    hidden,
    norm_gain,
    q_weight,
    k_weight,
    v_weight,
    o_weight,
    k_cache,
    v_cache,
    page_table,
    attend_list,
    lengths,
):
    highest = lax.Precision.HIGHEST
    mem_count = lax.axis_size("mem")
    mem_index = lax.axis_index("mem")
    feature_cols = norm_gain.shape[0]
    hidden_f = hidden.astype(jnp.float32)
    mean_sq = jnp.mean(hidden_f * hidden_f, axis=-1, keepdims=True)
    own_cols = lax.dynamic_slice_in_dim(hidden_f, mem_index * feature_cols, feature_cols, 1)
    normed = (own_cols * lax.rsqrt(mean_sq + EPSILON) * norm_gain.astype(jnp.float32)).astype(
        jnp.bfloat16
    )
    shard_piece = lax.all_gather(normed, "heads", axis=0, tiled=True)
    partial_value = jnp.concatenate(
        [
            jnp.dot(shard_piece, q_weight, preferred_element_type=jnp.float32),
            jnp.dot(shard_piece, k_weight, preferred_element_type=jnp.float32),
            jnp.dot(shard_piece, v_weight, preferred_element_type=jnp.float32),
        ],
        axis=1,
    )
    summed = lax.psum(partial_value, "mem")
    query_cols = q_weight.shape[1]
    value_cols = k_weight.shape[1]
    pool_blocks = k_cache.shape[0]
    local_kv = k_cache.shape[1]
    block_size = k_cache.shape[2]
    head_dim = k_cache.shape[3]
    row_count = lengths.shape[0]
    token_count = summed.shape[0]
    step_count = token_count // row_count
    local_heads = query_cols // head_dim
    per_kv = local_heads // local_kv
    query_count = step_count * per_kv
    scale_factor = head_dim ** (-0.5)
    queries = summed[:, :query_cols].astype(jnp.bfloat16)
    queries = queries.reshape(row_count, step_count, local_kv, per_kv, head_dim).transpose(
        0, 2, 1, 3, 4
    )
    queries = queries.reshape(row_count, local_kv, query_count, head_dim)
    new_keys = summed[:, query_cols : query_cols + value_cols].astype(jnp.bfloat16)
    new_keys = new_keys.reshape(row_count, step_count, local_kv, head_dim).transpose(0, 2, 1, 3)
    new_values = summed[:, query_cols + value_cols :].astype(jnp.bfloat16)
    new_values = new_values.reshape(row_count, step_count, local_kv, head_dim).transpose(0, 2, 1, 3)
    history = page_table.shape[1]
    pair_count = row_count * history
    block_ids = jnp.arange(history, dtype=jnp.int32)
    attended = jnp.any(attend_list[:, :, None] == block_ids[None, None, :], axis=1).reshape(
        pair_count
    )
    slot_global = mem_index * pool_blocks + jnp.arange(pool_blocks, dtype=jnp.int32)
    owner_hit = page_table.reshape(pair_count)[None, :] == slot_global[:, None]
    pair_of_slot = jnp.sum(
        jnp.where(owner_hit, jnp.arange(pair_count, dtype=jnp.int32)[None, :], 0), axis=1
    )
    slot_row = pair_of_slot // history
    slot_block = pair_of_slot % history
    slot_live = jnp.take(attended, pair_of_slot)
    capacity = 2 * row_count * attend_list.shape[1] // mem_count
    running_pos = jnp.cumsum(slot_live.astype(jnp.int32)) - 1
    picked = slot_live[None, :] & (
        running_pos[None, :] == jnp.arange(capacity, dtype=jnp.int32)[:, None]
    )
    chosen = jnp.sum(
        jnp.where(picked, jnp.arange(pool_blocks, dtype=jnp.int32)[None, :], 0), axis=1
    )
    block_keys = jnp.take(k_cache, chosen, axis=0)
    block_values = jnp.take(v_cache, chosen, axis=0)
    block_row = jnp.take(slot_row, chosen)
    block_index = jnp.take(slot_block, chosen)
    block_live = jnp.any(picked, axis=1)
    row_onehot = block_row[:, None] == jnp.arange(row_count, dtype=jnp.int32)[None, :]
    block_queries = jnp.take(queries, block_row, axis=0)
    scores = (
        jnp.einsum("cgqd,cgkd->cgqk", block_queries, block_keys, preferred_element_type=jnp.float32)
        * scale_factor
    )
    positions = block_index[:, None] * block_size + jnp.arange(block_size, dtype=jnp.int32)[None, :]
    valid = (block_live[:, None] & (positions < jnp.take(lengths, block_row)[:, None]))[
        :, None, None, :
    ]
    scores = jnp.where(valid, scores, NEG_FILL)
    block_peak = jnp.max(scores, axis=-1)
    row_peak = jnp.max(
        jnp.where(row_onehot[:, :, None, None], block_peak[:, None], NEG_FILL), axis=0
    )
    weights = jnp.where(
        valid, jnp.exp(scores - jnp.take(row_peak, block_row, axis=0)[..., None]), 0.0
    )
    weights_high = weights.astype(jnp.bfloat16)
    weights_low = (weights - weights_high.astype(jnp.float32)).astype(jnp.bfloat16)
    block_accum = jnp.einsum(
        "cgqk,cgkd->cgqd", weights_high, block_values, preferred_element_type=jnp.float32
    )
    block_accum = block_accum + jnp.einsum(
        "cgqk,cgkd->cgqd", weights_low, block_values, preferred_element_type=jnp.float32
    )
    onehot_f = row_onehot.astype(jnp.float32)
    row_sums = jnp.einsum("cr,cgq->rgq", onehot_f, jnp.sum(weights, axis=-1), precision=highest)
    row_accum = jnp.einsum("cr,cgqd->rgqd", onehot_f, block_accum, precision=highest)
    fresh_scores = (
        jnp.einsum("rgqd,rgtd->rgqt", queries, new_keys, preferred_element_type=jnp.float32)
        * scale_factor
    )
    causal = (
        jnp.arange(step_count, dtype=jnp.int32)[None, :]
        <= (jnp.arange(query_count, dtype=jnp.int32) // per_kv)[:, None]
    )
    fresh_scores = jnp.where(causal, fresh_scores, NEG_FILL)
    start_state = (
        jnp.full_like(row_peak, NEG_FILL),
        jnp.zeros_like(row_sums),
        jnp.zeros_like(row_accum),
    )
    cache_peak, cache_sum, cache_accum = fold_owners(
        start_state,
        (
            lax.all_gather(row_peak[None], "mem", axis=0, tiled=True),
            lax.all_gather(row_sums[None], "mem", axis=0, tiled=True),
            lax.all_gather(row_accum[None], "mem", axis=0, tiled=True),
        ),
    )
    final_peak = jnp.maximum(cache_peak, jnp.max(fresh_scores, axis=-1))
    carried = jnp.exp(cache_peak - final_peak)
    fresh_weights = jnp.where(causal, jnp.exp(fresh_scores - final_peak[..., None]), 0.0)
    final_sum = cache_sum * carried + jnp.sum(fresh_weights, axis=-1)
    final_accum = cache_accum * carried[..., None] + jnp.einsum(
        "rgqt,rgtd->rgqd", fresh_weights, new_values.astype(jnp.float32), precision=highest
    )
    attended_out = (final_accum / final_sum[..., None]).astype(jnp.bfloat16)
    attended_out = attended_out.reshape(
        row_count, local_kv, step_count, per_kv, head_dim
    ).transpose(0, 2, 1, 3, 4)
    attended_out = attended_out.reshape(token_count, query_cols)
    projected = lax.psum_scatter(
        jnp.dot(attended_out, o_weight, preferred_element_type=jnp.float32),
        "heads",
        scatter_dimension=0,
        tiled=True,
    )
    return projected.astype(jnp.bfloat16)


def solution(mesh):
    in_specs = (
        P(("groups", "heads"), None),
        P("mem"),
        P("mem", "heads"),
        P("mem", "heads"),
        P("mem", "heads"),
        P("heads", "mem"),
        P(("groups", "mem"), "heads", None, None),
        P(("groups", "mem"), "heads", None, None),
        P("groups", None),
        P("groups", None),
        P("groups"),
    )
    out_specs = P(("groups", "heads"), "mem")
    return jax.shard_map(shards, mesh=mesh, in_specs=in_specs, out_specs=out_specs, check_vma=False)
```

profile of v0, /device:TPU:0, one launch (start us, length us, event | category | flops | bytes accessed | tf_op | source)
XLA Modules:
  0.0 102.8 jit_solution(13370720556598059067)
XLA Ops:
  0.0 0.0 copy-start
  0.0 0.0 copy-start.1
  0.0 0.0 copy-start.6
  0.0 0.0 copy-start.7
  0.0 0.9 eq.60
  0.9 0.2 select_reduce_fusion.1
  1.2 0.8 fusion.34
  1.9 0.1 reshape.240
  2.0 0.8 gather_fusion
  2.8 0.1 copy.67
  2.9 0.1 reduce-window.8
  3.0 0.1 add_reduce_fusion
  3.1 0.1 select_reduce_fusion.2
  3.3 0.7 gather_fusion.5
  4.0 0.7 gather_fusion.4
  4.7 0.0 copy-done.1
  4.7 0.7 gather_fusion.1
  5.4 0.1 fusion.37
  5.6 0.1 fusion.38
  5.6 0.0 copy-done.6
  5.7 0.0 copy-done.7
  5.7 0.2 multiply_reduce_fusion
  5.9 0.1 fusion.35
  6.0 14.9 %all-gather.3 = bf16[4,4,2048]{2,1,0:T(4,128)(2,1)S(1)} all-gather(bf16[1,4,2048]{2,1,0:T(4,128)(2,1)S(1)} %fusion.35), channel_id=1, replica_groups=mesh['groups'=2,'mem'=4,'heads'=4] {'heads'}, dimensions={0}, use_global_device_ids=true | all-gather | bytes 81920 | tf_op jit(solution)/shard_map/all_gather | solution.py:43
  20.9 0.0 copy-start.3
  20.9 0.0 copy-start.4
  21.0 4.7 %fusion.62 = f32[16,2048]{1,0:T(8,128)S(1)} fusion(bf16[16,2048]{1,0:T(8,128)(2,1)S(1)} %reshape.322, bf16[2048,2048]{1,0:T(8,128)(2,1)} %param.17), kind=kOutput, calls=%fused_computation.117 | convolution fusion | flops 134217728 | bytes 8585216 | tf_op jit(solution)/shard_map/dot_general | solution.py:46
  25.7 0.0 copy-done.3
  25.7 0.3 fusion.63
  25.9 0.0 copy-done.4
  25.9 0.3 fusion.64
  26.2 11.7 %all-reduce.3 = bf16[16,2560]{1,0:T(8,128)(2,1)S(1)} all-reduce(f32[16,2560]{1,0:T(8,128)S(1)} %pad_maximum_fusion), channel_id=1, replica_groups=mesh['groups'=2,'mem'=4,'heads'=4] {'mem'}, use_global_device_ids=true, to_apply=%region_6.8 | all-reduce | flops 40960 | bytes 245760 | tf_op jit(solution)/shard_map/psum | solution.py:52
  38.0 1.3 %gather_fusion.2 = bf16[32,2,16,128]{3,2,1,0:T(8,128)(2,1)} fusion(bf16[8,2,16,128]{3,2,1,0:T(8,128)(2,1)S(1)} %bitcast.67, s32[1024]{0:T(1024)S(1)} %pad_clamp_fusion), kind=kCustom, calls=%fused_computation.6 | custom fusion | bytes 524416 | tf_op jit(solution)/shard_map/jit(_take)/gather | solution.py:103
  39.3 0.0 copy-done
  39.3 2.2 %gather_fusion.6 = bf16[32,2,128,128]{3,2,1,0:T(8,128)(2,1)} fusion(bf16[48,2,128,128]{3,2,1,0:T(8,128)(2,1)S(1)} %copy-done, s32[1024]{0:T(1024)S(1)} %pad_clamp_fusion.1), kind=kCustom, calls=%fused_computation.1.clone | custom fusion | bytes 4194432 | tf_op jit(solution)/shard_map/jit(_take)/gather | solution.py:97
  41.4 3.8 %fusion.60 = (f32[32,2,16]{2,1,0:T(2,128)S(1)}, f32[32,2,16,128]{3,2,1,0:T(8,128)}) fusion(bf16[32,2,128,128]{3,2,1,0:T(8,128)(2,1)} %gather_fusion.6, pred[32]{0:T(512)(128)(4,1)S(1)} %get-tuple-element.12, bf16[32,2,16,128]{3,2,1,0:T(8,128)(2,1)} %gather_fusion.2, pred[32]{0:T(512)(128)(4,1)S(1)} %get-tuple-element.14, pred[32,128]{1,0:T(8,128)(4,1)S(1)} %fusion.38), kind=kOutput, calls=%fused_computation.115 | convolution fusion | flops 35126272 | bytes 2891840 | tf_op jit(solution)/shard_map/cgqd,cgkd->cgqk/dot_general | solution.py:105
  45.2 0.1 copy.69
  45.3 0.1 select_reduce_fusion
  45.4 5.3 %all-gather.1 = f32[32,2,16]{2,1,0:T(2,128)S(1)} all-gather(f32[8,2,16]{2,1,0:T(2,128)S(1)} %select_reduce_fusion), channel_id=3, replica_groups=mesh['groups'=2,'mem'=4,'heads'=4] {'mem'}, dimensions={0}, use_global_device_ids=true | all-gather | bytes 5120 | tf_op jit(solution)/shard_map/all_gather | solution.py:148
  50.8 0.2 fusion.61
  51.1 0.6 gather_fusion.3
  51.7 0.1 broadcast_select_fusion.3
  51.8 1.4 %fusion.18 = f32[32,2,16]{2,1,0:T(2,128)S(1)} fusion(f32[32,2,16,128]{3,2,1,0:T(8,128)} %get-tuple-element.24, f32[32,2,16]{2,1,0:T(2,128)S(1)} %broadcast_select_fusion.3, pred[32,128]{1,0:T(8,128)(4,1)S(1)} %fusion.38), kind=kLoop, calls=%fused_computation.29 | loop fusion | flops 392192 | bytes 536576 | tf_op jit(solution)/shard_map/reduce_sum | solution.py:129
  53.3 0.1 fusion.31
  53.4 5.4 %all-gather.2 = f32[32,2,16]{2,0,1:T(8,128)S(1)} all-gather(f32[8,2,16]{2,0,1:T(8,128)S(1)} %fusion.31), channel_id=4, replica_groups=mesh['groups'=2,'mem'=4,'heads'=4] {'mem'}, dimensions={0}, use_global_device_ids=true | all-gather | bytes 5120 | tf_op jit(solution)/shard_map/all_gather | solution.py:149
  58.9 0.1 copy.73
  59.0 4.1 %gather_fusion.7 = bf16[32,2,128,128]{3,2,1,0:T(8,128)(2,1)} fusion(bf16[48,2,128,128]{3,2,1,0:T(8,128)(2,1)} %param.22, s32[1024]{0:T(1024)S(1)} %pad_clamp_fusion.1), kind=kCustom, calls=%fused_computation.3.clone | custom fusion | bytes 4194432 | tf_op jit(solution)/shard_map/jit(_take)/gather | solution.py:98
  63.0 0.0 copy-start.2
  63.0 0.0 copy-start.5
  63.0 2.6 %fusion.14 = f32[32,2,16,128]{3,2,1,0:T(8,128)S(1)} fusion(bf16[32,2,128,128]{3,2,1,0:T(8,128)(2,1)} %gather_fusion.7, pred[32]{0:T(512)(128)(4,1)S(1)} %get-tuple-element.12, f32[32,2,16,128]{3,2,1,0:T(8,128)} %get-tuple-element.24, f32[32,2,16]{2,1,0:T(2,128)S(1)} %broadcast_select_fusion.3, pred[32,128]{1,0:T(8,128)(4,1)S(1)} %fusion.38), kind=kOutput, calls=%fused_computation.22 | convolution fusion | flops 34996224 | bytes 3153952 | tf_op jit(solution)/shard_map/cgqk,cgkd->cgqd/dot_general | solution.py:122
  65.6 0.0 copy-done.2
  65.6 0.0 copy-done.5
  65.6 0.7 convolution_add_fusion
  66.4 0.6 fusion.16
  67.0 7.4 %all-gather = f32[32,2,16,128]{3,0,2,1:T(8,128)S(1)} all-gather(f32[8,2,16,128]{3,0,2,1:T(8,128)S(1)} %fusion.16), channel_id=2, replica_groups=mesh['groups'=2,'mem'=4,'heads'=4] {'mem'}, dimensions={0}, use_global_device_ids=true | all-gather | bytes 655360 | tf_op jit(solution)/shard_map/all_gather | solution.py:150
  74.4 0.2 fusion.15
  74.6 0.3 fusion.11
  75.0 0.0 copy-start.8
  75.0 4.6 %fusion.65 = f32[16,2048]{1,0:T(8,128)S(1)} fusion(bf16[16,2048]{1,0:T(8,128)(2,1)S(1)} %reshape.246, bf16[2048,2048]{1,0:T(8,128)(2,1)} %param.20), kind=kOutput, calls=%fused_computation.120 | convolution fusion | flops 134217728 | bytes 8585216 | tf_op jit(solution)/shard_map/dot_general | solution.py:166
  79.6 21.4 %all-reduce.4 = bf16[16,2048]{1,0:T(8,128)(2,1)S(1)} all-reduce(f32[16,2048]{1,0:T(8,128)S(1)} %fusion.65), channel_id=5, replica_groups=mesh['groups'=2,'mem'=4,'heads'=4] {'heads'}, use_global_device_ids=true, to_apply=%region_15.18.clone | all-reduce | flops 32768 | bytes 196608
  101.0 0.0 copy-done.8
  101.0 0.6 dynamic-slice
  102.2 0.6 dynamic-slice_convert_fusion
  (34 shorter events, 0.4 us)
Async XLA Ops:
  0.0 39.3 %copy-start = (bf16[48,2,128,128]{3,2,1,0:T(8,128)(2,1)S(1)}, bf16[48,2,128,128]{3,2,1,0:T(8,128)(2,1)}, u32[]{:S(2)}) copy-start(bf16[48,2,128,128]{3,2,1,0:T(8,128)(2,1)} %param.21) | copy-start | bytes 9437188
  0.0 4.7 %copy-start.1 = (s32[8]{0:T(128)S(1)}, s32[8]{0:T(128)}, u32[]{:S(2)}) copy-start(s32[8]{0:T(128)} %param.25) | copy-start | bytes 100
  0.0 5.6 %copy-start.6 = (bf16[4,8192]{1,0:T(4,128)(2,1)S(1)}, bf16[4,8192]{1,0:T(4,128)(2,1)}, u32[]{:S(2)}) copy-start(bf16[4,8192]{1,0:T(4,128)(2,1)} %param.15) | copy-start | bytes 196612
  0.0 5.7 %copy-start.7 = (bf16[2048]{0:T(1024)(128)(2,1)S(1)}, bf16[2048]{0:T(1024)(128)(2,1)}, u32[]{:S(2)}) copy-start(bf16[2048]{0:T(1024)(128)(2,1)} %param.16) | copy-start | bytes 12292
  20.9 4.7 %copy-start.3 = (bf16[2048,256]{1,0:T(8,128)(2,1)S(1)}, bf16[2048,256]{1,0:T(8,128)(2,1)}, u32[]{:S(2)}) copy-start(bf16[2048,256]{1,0:T(8,128)(2,1)} %param.18) | copy-start | bytes 3145732
  20.9 5.0 %copy-start.4 = (bf16[2048,256]{1,0:T(8,128)(2,1)S(1)}, bf16[2048,256]{1,0:T(8,128)(2,1)}, u32[]{:S(2)}) copy-start(bf16[2048,256]{1,0:T(8,128)(2,1)} %param.19) | copy-start | bytes 3145732
  63.0 2.6 %copy-start.2 = (bf16[32,2,128,128]{3,2,1,0:T(8,128)(2,1)S(1)}, bf16[32,2,128,128]{3,2,1,0:T(8,128)(2,1)}, u32[]{:S(2)}) copy-start(bf16[32,2,128,128]{3,2,1,0:T(8,128)(2,1)} %gather_fusion.7) | copy-start | bytes 6291460
  63.0 2.6 %copy-start.5 = (f32[32,2,16,128]{3,2,1,0:T(8,128)S(1)}, f32[32,2,16,128]{3,2,1,0:T(8,128)}, u32[]{:S(2)}) copy-start(f32[32,2,16,128]{3,2,1,0:T(8,128)} %get-tuple-element.24) | copy-start | bytes 1572868
  75.0 26.0 %copy-start.8 = (u32[32]{0:T(128)S(1)}, u32[32]{0:T(128)}, u32[]{:S(2)}) copy-start(u32[32]{0:T(128)} %constant.151) | copy-start | bytes 388
where the time goes:
time: 103 us
  blocking collectives  66.2 us (64%)
  matrix products  18.2 us (18%)
  local copies, waits for them, and re-layouts  13.6 us (13%)
  other arithmetic  3.86 us (4%)
    unnamed x1, blocking collectives  21.4 us
    all_gather x1, blocking collectives, shards(): shard_piece = lax.all_gather(normed, 'heads', axis=0, tiled=True)  14.9 us
    psum x1, blocking collectives, shards(): summed = lax.psum(partial_value, 'mem')  11.7 us
    all_gather x1, blocking collectives, shards(): lax.all_gather(row_accum[None], 'mem', axis=0, tiled=True)  7.38 us
    all_gather x1, blocking collectives, shards(): lax.all_gather(row_sums[None], 'mem', axis=0, tiled=True)  5.43 us
    all_gather x1, blocking collectives, shards(): lax.all_gather(row_peak[None], 'mem', axis=0, tiled=True)  5.32 us
    dot_general x1, matrix products, shards(): jnp.dot(shard_piece, q_weight, preferred_element_type=jnp.float32)  4.72 us
    dot_general x1, matrix products, shards(): jnp.dot(attended_out, o_weight, preferred_element_type=jnp.float32)  4.58 us

commit v1 on v0

--- a/solution.py
+++ b/solution.py
@@ -5,6 +5,17 @@
 
 NEG_FILL = -1e30
 EPSILON = 1e-05
+
+
+def pass_along(x, axis, dim):
+    size = lax.axis_size(axis)
+    route = [(i, (i + 1) % size) for i in range(size)]
+    terms = [x]
+    for stride in range(1, size):
+        terms = [lax.ppermute(terms[0], axis, route), *terms]
+    out = jnp.concatenate(terms, axis=dim)
+    shift = (lax.axis_index(axis) + 1) * terms[-1].shape[dim]
+    return jnp.roll(out, shift, axis=dim)
 
 
 def fold_owners(running, shard_piece):
@@ -40,7 +51,7 @@
     normed = (own_cols * lax.rsqrt(mean_sq + EPSILON) * norm_gain.astype(jnp.float32)).astype(
         jnp.bfloat16
     )
-    shard_piece = lax.all_gather(normed, "heads", axis=0, tiled=True)
+    shard_piece = pass_along(normed, "heads", 0)
     partial_value = jnp.concatenate(
         [
             jnp.dot(shard_piece, q_weight, preferred_element_type=jnp.float32),

time: 103 us -> 105 us (1.019)
  blocking collectives: 66.2 us -> 52 us
  other arithmetic: 3.86 us -> 10.3 us
  starting transfers between devices: 0 us -> 4.68 us
  waiting for transfers between devices: 0 us -> 3.96 us
  matrix products: 18.2 us -> 19.3 us
    all_gather x1 -> x0, blocking collectives: 14.9 us -> none  [shards(): shard_piece = lax.all_gather(normed, 'heads', axis=0, tiled=True)]
    ppermute x0 -> x3, starting transfers between devices: none -> 4.68 us  [pass_along(): terms = [lax.ppermute(terms[0], axis, route), *terms]]
    ppermute x0 -> x3, waiting for transfers between devices: none -> 3.96 us  [pass_along(): terms = [lax.ppermute(terms[0], axis, route), *terms]]
    reduce_sum x1, other arithmetic: 0.2 us -> 1.25 us  [fold_owners(): joint_accum = jnp.sum(piece_accum * piece_factor[..., None], axis=0)]
  transfers between devices with their start and end apart: 0 -> 3, of which waited for: 0 -> 1; matrix products, arithmetic and copies ran while one was open for 0% -> 14% of each run, Pallas kernels for 0% -> 0%
where the time goes in v1:
time: 105 us; the launch traced here: 104 us
  blocking collectives  52 us (50%)
  matrix products  19.3 us (18%)
  local copies, waits for them, and re-layouts  13.1 us (12%)
  other arithmetic  10.3 us (10%)
  starting transfers between devices  4.68 us (4%)
  waiting for transfers between devices  3.96 us (4%)
    unnamed x1, blocking collectives  21.7 us
    psum x1, blocking collectives, shards(): summed = lax.psum(partial_value, 'mem')  11.7 us
    all_gather x1, blocking collectives, shards(): lax.all_gather(row_accum[None], 'mem', axis=0, tiled=True)  7.83 us
    all_gather x1, blocking collectives, shards(): lax.all_gather(row_sums[None], 'mem', axis=0, tiled=True)  5.43 us
    all_gather x1, blocking collectives, shards(): lax.all_gather(row_peak[None], 'mem', axis=0, tiled=True)  5.32 us
    dot_general x1, matrix products, shards(): jnp.dot(shard_piece, q_weight, preferred_element_type=jnp.float32)  4.73 us
    ppermute x3, starting transfers between devices, pass_along(): terms = [lax.ppermute(terms[0], axis, route), *terms]  4.68 us
    dot_general x1, matrix products, shards(): jnp.dot(attended_out, o_weight, preferred_element_type=jnp.float32)  4.58 us
  transfers between devices with their start and end apart: 3, of which 1 were waited for; matrix products, arithmetic and copies ran while one was open for 14% of the time, Pallas kernels for 0%

profile of v1, /device:TPU:0, one launch (start us, length us, event | category | flops | bytes accessed | tf_op | source)
XLA Modules:
  0.0 104.4 jit_solution(16197226178615395177)
XLA Ops:
  0.0 0.0 copy-start
  0.0 1.0 convert_element_type.42
  1.0 1.0 multiply_reduce_fusion
  2.0 0.7 convert_element_type.43
  2.7 0.1 multiply_convert_fusion
  2.8 3.1 %collective-permute-start = (bf16[4,2048]{1,0:T(4,128)(2,1)S(1)}, bf16[4,2048]{1,0:T(4,128)(2,1)S(1)}, u32[]{:S(2)}, u32[]{:S(2)}) collective-permute-start(bf16[4,2048]{1,0:T(4,128)(2,1)S(1)} %multiply_convert_fusion), channel_id=1, source_target_pairs={{0,1},{1,2},{2,3},{3,0},{4,5},{5,6},{6,7},{7,4},{8,9},{9,10},{10,1... | collective-permute-start | bytes 49160 | tf_op jit(solution)/shard_map/ppermute | solution.py:15
  5.9 0.8 eq.63
  6.7 0.2 select_reduce_fusion.1
  6.9 0.8 fusion.40
  7.7 0.1 reshape.240
  7.8 0.8 gather_fusion
  8.6 0.1 copy.67
  8.7 0.1 reduce-window.8
  8.8 0.1 add_reduce_fusion
  8.9 0.1 select_reduce_fusion.2
  9.0 0.1 fusion.42
  9.2 0.7 gather_fusion.5
  9.9 0.7 gather_fusion.4
  10.6 0.0 copy-done.10
  10.6 0.0 copy-start.9
  10.6 0.7 gather_fusion.1
  11.3 0.5 broadcast_select_fusion.4
  11.9 0.7 fusion.43
  12.5 0.6 iota_compare_fusion.2
  13.1 0.0 collective-permute-done
  13.1 1.6 %collective-permute-start.1 = (bf16[4,2048]{1,0:T(4,128)(2,1)S(1)}, bf16[4,2048]{1,0:T(4,128)(2,1)S(1)}, u32[]{:S(2)}, u32[]{:S(2)}) collective-permute-start(bf16[4,2048]{1,0:T(4,128)(2,1)S(1)} %collective-permute-done), channel_id=1, source_target_pairs={{0,1},{1,2},{2,3},{3,0},{4,5},{5,6},{6,7},{7,4},{8,9},{9,10},{10,1... | collective-permute-start | bytes 49160 | tf_op jit(solution)/shard_map/ppermute | solution.py:15
  14.7 4.0 %collective-permute-done.1 = bf16[4,2048]{1,0:T(4,128)(2,1)S(1)} collective-permute-done((bf16[4,2048]{1,0:T(4,128)(2,1)S(1)}, bf16[4,2048]{1,0:T(4,128)(2,1)S(1)}, u32[]{:S(2)}, u32[]{:S(2)}) %collective-permute-start.1) | collective-permute-done | bytes 16416 | tf_op jit(solution)/shard_map/ppermute | solution.py:15
  18.7 0.0 collective-permute-start.2
  18.7 0.6 iota_compare_fusion.5
  19.2 2.1 %gather_fusion.6 = bf16[32,2,128,128]{3,2,1,0:T(8,128)(2,1)} fusion(bf16[48,2,128,128]{3,2,1,0:T(8,128)(2,1)S(1)} %copy-done, s32[1024]{0:T(1024)S(1)} %pad_clamp_fusion.1), kind=kCustom, calls=%fused_computation.1.clone | custom fusion | bytes 4194432 | tf_op jit(solution)/shard_map/jit(_take)/gather | solution.py:108
  21.3 0.0 copy-done.9
  21.4 4.1 %gather_fusion.7 = bf16[32,2,128,128]{3,2,1,0:T(8,128)(2,1)} fusion(bf16[48,2,128,128]{3,2,1,0:T(8,128)(2,1)} %param.22, s32[1024]{0:T(1024)S(1)} %pad_clamp_fusion.1), kind=kCustom, calls=%fused_computation.3.clone | custom fusion | bytes 4194432 | tf_op jit(solution)/shard_map/jit(_take)/gather | solution.py:109
  25.4 0.6 dynamic-slice
  26.6 0.0 collective-permute-done.2
  26.6 0.1 concatenate.9
  26.8 0.0 copy-start.3
  26.8 0.0 copy-start.4
  26.8 4.7 %fusion.34 = f32[16,2048]{1,0:T(8,128)S(1)} fusion(bf16[2048,2048]{1,0:T(8,128)(2,1)} %param.17, bf16[32,2048]{1,0:T(8,128)(2,1)S(1)} %concatenate.9, s32[]{:T(128)S(6)} %select_n.160), kind=kOutput, calls=%fused_computation.51 | convolution fusion | flops 134217728 | bytes 8585220 | tf_op jit(solution)/shard_map/dot_general | solution.py:57
  31.5 0.3 fusion.30
  31.8 0.3 fusion.32
  32.1 11.7 %all-reduce.3 = bf16[16,2560]{1,0:T(8,128)(2,1)S(1)} all-reduce(f32[16,2560]{1,0:T(8,128)S(1)} %pad_maximum_fusion), channel_id=1, replica_groups=mesh['groups'=2,'mem'=4,'heads'=4] {'mem'}, use_global_device_ids=true, to_apply=%region_6.8 | all-reduce | flops 40960 | bytes 245760 | tf_op jit(solution)/shard_map/psum | solution.py:63
  43.9 0.7 gather_fusion.2
  44.6 3.7 %fusion.68 = (f32[32,2,16]{2,1,0:T(2,128)S(1)}, f32[32,2,16,128]{3,2,1,0:T(8,128)}) fusion(bf16[32,2,128,128]{3,2,1,0:T(8,128)(2,1)} %gather_fusion.6, pred[32]{0:T(512)(128)(4,1)} %copy-done.10, bf16[32,2,16,128]{3,2,1,0:T(8,128)(2,1)S(1)} %gather_fusion.2, pred[32]{0:T(512)(128)(4,1)} %get-tuple-element.14, pred[32,128]{1,0:T(8,128)(4,1)} %fusion.43), kind=kOutput, calls=%fused_computation.123 | convolution fusion | flops 35126272 | bytes 2891840 | tf_op jit(solution)/shard_map/cgqd,cgkd->cgqk/dot_general | solution.py:116
  48.3 0.1 copy.69
  48.4 0.1 select_reduce_fusion
  48.5 5.3 %all-gather.1 = f32[32,2,16]{2,1,0:T(2,128)S(1)} all-gather(f32[8,2,16]{2,1,0:T(2,128)S(1)} %select_reduce_fusion), channel_id=3, replica_groups=mesh['groups'=2,'mem'=4,'heads'=4] {'mem'}, dimensions={0}, use_global_device_ids=true | all-gather | bytes 5120 | tf_op jit(solution)/shard_map/all_gather | solution.py:159
  53.8 0.7 gather_fusion.3
  54.6 0.8 fusion.69
  55.4 0.7 broadcast_select_fusion.3
  56.2 1.4 %fusion.18 = f32[32,2,16]{2,1,0:T(2,128)S(1)} fusion(f32[32,2,16,128]{3,2,1,0:T(8,128)} %get-tuple-element.24, f32[32,2,16]{2,1,0:T(2,128)S(1)} %broadcast_select_fusion.3, pred[32,128]{1,0:T(8,128)(4,1)} %fusion.43), kind=kLoop, calls=%fused_computation.29 | loop fusion | flops 392192 | bytes 536576 | tf_op jit(solution)/shard_map/reduce_sum | solution.py:140
  57.6 0.7 fusion.37
  58.3 5.4 %all-gather.2 = f32[32,2,16]{2,0,1:T(8,128)S(1)} all-gather(f32[8,2,16]{2,0,1:T(8,128)S(1)} %fusion.37), channel_id=4, replica_groups=mesh['groups'=2,'mem'=4,'heads'=4] {'mem'}, dimensions={0}, use_global_device_ids=true | all-gather | bytes 5120 | tf_op jit(solution)/shard_map/all_gather | solution.py:160
  63.8 0.1 copy.73
  63.9 2.6 %fusion.14 = f32[32,2,16,128]{3,2,1,0:T(8,128)S(1)} fusion(bf16[32,2,128,128]{3,2,1,0:T(8,128)(2,1)} %gather_fusion.7, pred[32]{0:T(512)(128)(4,1)} %copy-done.10, f32[32,2,16,128]{3,2,1,0:T(8,128)} %get-tuple-element.24, f32[32,2,16]{2,1,0:T(2,128)S(1)} %broadcast_select_fusion.3, pred[32,128]{1,0:T(8,128)(4,1)} %fusion.43), kind=kOutput, calls=%fused_computation.22 | convolution fusion | flops 34996224 | bytes 3153952 | tf_op jit(solution)/shard_map/cgqk,cgkd->cgqd/dot_general | solution.py:133
  66.5 0.0 copy-done.2
  66.5 0.0 copy-done.6
  66.6 0.7 convolution_add_fusion
  67.3 0.6 fusion.16
  67.9 7.8 %all-gather = f32[32,2,16,128]{3,0,2,1:T(8,128)} all-gather(f32[8,2,16,128]{3,0,2,1:T(8,128)S(1)} %fusion.16), channel_id=2, replica_groups=mesh['groups'=2,'mem'=4,'heads'=4] {'mem'}, dimensions={0}, use_global_device_ids=true | all-gather | bytes 655360 | tf_op jit(solution)/shard_map/all_gather | solution.py:161
  75.8 1.3 %fusion.15 = f32[8,2,16,128]{3,0,2,1:T(8,128)S(1)} fusion(f32[32,2,16,128]{3,0,2,1:T(8,128)} %all-gather, f32[4,8,2,16]{1,0,3,2:T(4,128)S(1)} %copy.73), kind=kLoop, calls=%fused_computation.24 | loop fusion | flops 229376 | bytes 659456 | tf_op jit(solution)/shard_map/reduce_sum | solution.py:27
  77.1 0.3 fusion.11
  77.5 4.6 %fusion.70 = f32[16,2048]{1,0:T(8,128)S(1)} fusion(bf16[16,2048]{1,0:T(8,128)(2,1)S(1)} %reshape.246, bf16[2048,2048]{1,0:T(8,128)(2,1)} %param.20), kind=kOutput, calls=%fused_computation.125 | convolution fusion | flops 134217728 | bytes 8585216 | tf_op jit(solution)/shard_map/dot_general | solution.py:177
  82.1 21.7 %all-reduce.4 = bf16[16,2048]{1,0:T(8,128)(2,1)S(1)} all-reduce(f32[16,2048]{1,0:T(8,128)S(1)} %fusion.70), channel_id=5, replica_groups=mesh['groups'=2,'mem'=4,'heads'=4] {'heads'}, use_global_device_ids=true, to_apply=%region_15.18.clone | all-reduce | flops 32768 | bytes 196608
  103.8 0.6 dynamic-slice_convert_fusion
  (50 shorter events, 0.4 us)
Async XLA Ops:
  0.0 19.2 %copy-start = (bf16[48,2,128,128]{3,2,1,0:T(8,128)(2,1)S(1)}, bf16[48,2,128,128]{3,2,1,0:T(8,128)(2,1)}, u32[]{:S(2)}) copy-start(bf16[48,2,128,128]{3,2,1,0:T(8,128)(2,1)} %param.21) | copy-start | bytes 9437188
  0.0 10.6 %copy-start.1 = (s32[8]{0:T(128)S(1)}, s32[8]{0:T(128)}, u32[]{:S(2)}) copy-start(s32[8]{0:T(128)} %param.25) | copy-start | bytes 100
  2.8 10.3 %collective-permute-start = (bf16[4,2048]{1,0:T(4,128)(2,1)S(1)}, bf16[4,2048]{1,0:T(4,128)(2,1)S(1)}, u32[]{:S(2)}, u32[]{:S(2)}) collective-permute-start(bf16[4,2048]{1,0:T(4,128)(2,1)S(1)} %multiply_convert_fusion), channel_id=1, source_target_pairs={{0,1},{1,2},{2,3},{3,0},{4,5},{5,6},{6,7},{7,4},{8,9},{9,10},{10,1... | collective-permute-start | bytes 49160 | tf_op jit(solution)/shard_map/ppermute | solution.py:15
  9.9 0.7 copy-start.10
  10.6 10.8 %copy-start.7 = (s32[32]{0:T(128)}, s32[32]{0:T(128)S(1)}, u32[]{:S(2)}) copy-start(s32[32]{0:T(128)S(1)} %get-tuple-element.16) | copy-start | bytes 388
  10.6 10.7 %copy-start.9 = (s32[1024]{0:T(1024)}, s32[1024]{0:T(1024)S(1)}, u32[]{:S(2)}) copy-start(s32[1024]{0:T(1024)S(1)} %pad_clamp_fusion) | copy-start | bytes 12292
  13.1 5.5 %collective-permute-start.1 = (bf16[4,2048]{1,0:T(4,128)(2,1)S(1)}, bf16[4,2048]{1,0:T(4,128)(2,1)S(1)}, u32[]{:S(2)}, u32[]{:S(2)}) collective-permute-start(bf16[4,2048]{1,0:T(4,128)(2,1)S(1)} %collective-permute-done), channel_id=1, source_target_pairs={{0,1},{1,2},{2,3},{3,0},{4,5},{5,6},{6,7},{7,4},{8,9},{9,10},{10,1... | collective-permute-start | bytes 49160 | tf_op jit(solution)/shard_map/ppermute | solution.py:15
  18.7 8.0 %collective-permute-start.2 = (bf16[4,2048]{1,0:T(4,128)(2,1)S(1)}, bf16[4,2048]{1,0:T(4,128)(2,1)S(1)}, u32[]{:S(2)}, u32[]{:S(2)}) collective-permute-start(bf16[4,2048]{1,0:T(4,128)(2,1)S(1)} %collective-permute-done.1), channel_id=1, source_target_pairs={{0,1},{1,2},{2,3},{3,0},{4,5},{5,6},{6,7},{7,4},{8,9},{9,10},{10,1... | collective-permute-start | bytes 49160 | tf_op jit(solution)/shard_map/ppermute | solution.py:15
  21.3 4.1 %copy-start.14 = (u32[32]{0:T(128)S(1)}, u32[32]{0:T(128)}, u32[]{:S(2)}) copy-start(u32[32]{0:T(128)} %constant.176) | copy-start | bytes 388
  26.8 4.8 %copy-start.3 = (bf16[2048,256]{1,0:T(8,128)(2,1)S(1)}, bf16[2048,256]{1,0:T(8,128)(2,1)}, u32[]{:S(2)}) copy-start(bf16[2048,256]{1,0:T(8,128)(2,1)} %param.19) | copy-start | bytes 3145732
  26.8 5.0 %copy-start.4 = (bf16[2048,256]{1,0:T(8,128)(2,1)S(1)}, bf16[2048,256]{1,0:T(8,128)(2,1)}, u32[]{:S(2)}) copy-start(bf16[2048,256]{1,0:T(8,128)(2,1)} %param.18) | copy-start | bytes 3145732
  44.6 3.8 %copy-start.12 = (pred[32,8]{0,1:T(8,128)(4,1)S(1)}, pred[32,8]{0,1:T(8,128)(4,1)}, u32[]{:S(2)}) copy-start(pred[32,8]{0,1:T(8,128)(4,1)} %iota_compare_fusion.2) | copy-start | bytes 772
  63.9 2.7 %copy-start.2 = (bf16[32,2,128,128]{3,2,1,0:T(8,128)(2,1)S(1)}, bf16[32,2,128,128]{3,2,1,0:T(8,128)(2,1)}, u32[]{:S(2)}) copy-start(bf16[32,2,128,128]{3,2,1,0:T(8,128)(2,1)} %gather_fusion.7) | copy-start | bytes 6291460
  63.9 2.7 %copy-start.5 = (f32[32,2,16,128]{3,2,1,0:T(8,128)S(1)}, f32[32,2,16,128]{3,2,1,0:T(8,128)}, u32[]{:S(2)}) copy-start(f32[32,2,16,128]{3,2,1,0:T(8,128)} %get-tuple-element.24) | copy-start | bytes 1572868
  63.9 2.7 %copy-start.6 = (pred[32,128]{1,0:T(8,128)(4,1)S(1)}, pred[32,128]{1,0:T(8,128)(4,1)}, u32[]{:S(2)}) copy-start(pred[32,128]{1,0:T(8,128)(4,1)} %fusion.43) | copy-start | bytes 12292
  63.9 2.7 %copy-start.11 = (pred[32]{0:T(512)(128)(4,1)S(1)}, pred[32]{0:T(512)(128)(4,1)}, u32[]{:S(2)}) copy-start(pred[32]{0:T(512)(128)(4,1)} %copy-done.10) | copy-start | bytes 100
  66.6 0.8 copy-start.8
  66.6 9.2 %copy-start.13 = (pred[16,2]{0,1:T(4,128)(4,1)S(1)}, pred[16,2]{0,1:T(4,128)(4,1)}, u32[]{:S(2)}) copy-start(pred[16,2]{0,1:T(4,128)(4,1)} %iota_compare_fusion.5) | copy-start | bytes 100
